TPU v7x, 128 devices: a whole 4x4x4 slice. The times are simulated.
128 devices in a mesh: gx: 16 (over x, z), gy: 8 (over y, core).
Axes of the slice: x: 4, y: 4, z: 4, core: 2. Of those that a mesh axis runs over, the one named last changes fastest.
Arguments:
- particles: float32 [4, 262144], P(None, ('gx', 'gy')), may hold values from -1 to 1, as said below
- tree_cells: float32 [10, 1048576], P(None, ('gx', 'gy')), may hold values from -1 to 1, as said below
- let_list: int32 [128, 128, 4], P(('gx', 'gy')), may hold values from 0 to 63
- let_count: int32 [128, 128], P(('gx', 'gy')), may hold values from 1 to 4, as said below
- part_list: int32 [128, 4, 4], P(('gx', 'gy')), may hold values from 0 to 15
- cell_lists: int32 [2048, 16], P(('gx', 'gy')), may hold values from 0 to 575
- near_lists: int32 [2048, 8], P(('gx', 'gy')), may hold values from 0 to 31
Outputs:
- forces: float32 [4, 262144], P(None, ('gx', 'gy'))
Inputs may be any that keep to these rules, and one draw needn't show every extreme that they name: let_count is 4 wherever sender and receiver are at most 2 apart along gx+gy, and between 1 and 4 elsewhere. `particles`: positions lie in [-1, 1], masses are positive. `tree_cells`: centres lie in [-1, 1], masses are positive, the quadrupole is traceless.
All inputs are finite; a program needn't handle non-finite values.
Results may differ from a plain program's by a relative error of at most 0.0003.
Values sent between devices are 32-bit elements; how exact they have to be, the bound alone decides.
A program may use at most 64 MiB of HBM per device.

v0:
```python
import jax
import jax.numpy as jnp
from jax import lax
from jax.experimental import pallas as pl
from jax.experimental.pallas import tpu as pltpu
from jax.sharding import PartitionSpec as P

BLK = 128
NBLK = 16
NCB = 64
DEV = 128
LC = 16
LP = 8
ROWS = 9
EPS = 0.0025
MESH = pl.DeviceIdType.MESH
near_offsets = (1, -1, 2, -2)

OWN = NCB * ROWS
ZERO = OWN + DEV * ROWS
ROWS0 = ZERO + ROWS
ONE = ROWS + 1
ROWS1 = DEV * ONE
LATE = 2 * ROWS
ROWS2 = DEV * LATE
N0 = 4
N1 = 4
NEAR_FIRST = 4

f32 = jnp.float32
i32 = jnp.int32


def rows_of(ref, first, count):
    return [jnp.broadcast_to(ref[first + r], (8, BLK)) for r in range(count)]


def rows_of_two(pool0, pool1, entry):
    other = entry >= ROWS0
    first0 = jnp.where(other, 0, entry)
    first1 = jnp.where(other, entry - ROWS0, 0)
    return [
        jnp.broadcast_to(jnp.where(other, pool1[first1 + r], pool0[first0 + r]), (8, BLK))
        for r in range(ROWS)
    ]


def cell_item(t_ref, t_base, sources, acc):
    def tile(t, carry):
        s = pl.ds(pl.multiple_of(t * 8, 8), 8)
        tx, ty, tz = t_ref[t_base, s], t_ref[t_base + 1, s], t_ref[t_base + 2, s]
        sums = [acc[k, s] for k in range(4)]
        for X, Y, Z, M, Qxx, Qyy, Qxy, Qxz, Qyz in sources:
            x = tx - X
            y = ty - Y
            z = tz - Z
            u = lax.rsqrt(x * x + y * y + z * z + EPS)
            u2 = u * u
            u5 = u * u2 * u2
            x5 = u5 * x
            y5 = u5 * y
            z5 = u5 * z
            qx = Qxx * x5 + Qxy * y5 + Qxz * z5
            qy = Qxy * x5 + Qyy * y5 + Qyz * z5
            qz = Qxz * x5 + Qyz * y5 - (Qxx + Qyy) * z5
            w = x * qx + y * qy + z * qz
            mu = M * u
            p = u2 * (mu + 2.5 * w)
            for k, term in enumerate((p * x - qx, p * y - qy, p * z - qz, mu + 0.5 * w)):
                sums[k] = sums[k] + term
        for k in range(4):
            acc[k, s] = sums[k]
        return carry

    lax.fori_loop(0, 16, tile, 0, unroll=True)


def cell_items(count, rows_at, t_ref, t_base, acc):
    def pair(i, carry):
        cell_item(t_ref, t_base, [rows_at(2 * i), rows_at(2 * i + 1)], acc)
        return carry

    def single(i, carry):
        cell_item(t_ref, t_base, [rows_at(i)], acc)
        return carry

    pairs = count // 2 if isinstance(count, int) else count >> 1
    lax.fori_loop(0, pairs, pair, 0)
    if not isinstance(count, int) or count % 2:
        lax.fori_loop(2 * pairs, count, single, 0)


def near_item(t_ref, t_base, pool, blocks, acc):
    sources = [rows_of(pool, block * 4, 4) for block in blocks]

    def tile(t, carry):
        s = pl.ds(pl.multiple_of(t * 8, 8), 8)
        tx, ty, tz = t_ref[t_base, s], t_ref[t_base + 1, s], t_ref[t_base + 2, s]
        sums = [acc[k, s] for k in range(4)]
        for X, Y, Z, M in sources:
            x = tx - X
            y = ty - Y
            z = tz - Z
            u = lax.rsqrt(x * x + y * y + z * z + EPS)
            mu = M * u
            p = mu * (u * u)
            for k, term in enumerate((p * x, p * y, p * z, mu)):
                sums[k] = sums[k] + term
        for k in range(4):
            acc[k, s] = sums[k]
        return carry

    lax.fori_loop(0, 16, tile, 0, unroll=True)


def lane_totals(acc):
    lane = lax.broadcasted_iota(i32, (BLK, BLK), 1)
    packed = jnp.zeros((BLK, BLK), f32)
    for k in range(4):
        total = jnp.sum(acc[k], axis=1, keepdims=True)
        packed = jnp.where(lane == k, jnp.broadcast_to(total, (BLK, BLK)), packed)
    return -jnp.transpose(packed)[:8]


def ranks(flags, lane):
    rank = flags.astype(i32)
    for shift in (1, 2, 4, 8):
        rank = rank + jnp.where(lane >= shift, pltpu.roll(rank, shift, 1), 0)
    return rank


def nth(flags, rank, n, values):
    return jnp.sum(jnp.where(flags & (rank == n), values, 0), axis=1, keepdims=True)


def exchange_kernel(
    let_in, count_in, part_in, near_in, cell_in, parts_in, cells_in,
    acc, t_ref, pool0, pool1, pool2, left_lists,
    let_list, let_count, part_list, near_lists, cell_lists, cell_ids,
    cells, parts, own_cells, own_rows, chosen0, chosen1, chosen2, npick, npool,
    ids_v, count_v, list_v, list0, list1,
    send_sem, recv_sem, send_n, recv_n, local_sem,
):
    gx = lax.axis_index("gx")
    gy = lax.axis_index("gy")
    me = gx * 8 + gy
    cx, cz = gx // 4, lax.rem(gx, 4)
    cy, cc = gy // 2, lax.rem(gy, 2)
    px = [lax.rem(cx + m, 4) * 4 for m in range(4)]
    py = [lax.rem(cy + m, 4) * 2 for m in range(4)]

    def to_all(action):
        def batch(h, carry, skip=False):
            pz = [lax.rem(cz + h + m, 4) for m in range(4)]
            core = lax.rem(cc + h // 4, 2)
            for b in range(4):
                for a in range(4):
                    if skip and a == 0 and b == 0:
                        continue
                    dy = (a + b) % 4
                    action(px[a] + pz[(2 * a + dy) % 4], py[dy] + core)
            return carry

        batch(0, 0, True)
        lax.fori_loop(1, 8, batch, 0)

    barrier = pltpu.get_barrier_semaphore()

    pz_all = [lax.rem(cz + m, 4) for m in range(4)]
    cores = [cc, 1 - cc]
    hops = (0, 1, 2, 1)
    steps = [
        (hops[dx] + hops[dy] + hops[dz], dx, dy, dz, dc)
        for dx in range(4)
        for dy in range(4)
        for dz in range(4)
        for dc in range(2)
    ]

    def greet_all():
        for far, dx, dy, dz, dc in sorted(steps, reverse=True)[:-1]:
            pl.semaphore_signal(
                barrier,
                inc=1,
                device_id=(px[dx] + pz_all[dz], py[dy] + cores[dc]),
                device_id_type=MESH,
            )

    loads = [
        pltpu.make_async_copy(source, target, local_sem.at[n])
        for n, (source, target) in enumerate(
            (
                (cells_in, cells),
                (parts_in, parts),
                (let_in, let_list),
                (count_in, let_count),
                (part_in, part_list),
                (near_in, near_lists),
                (cell_in, cell_lists),
                (cell_in, cell_ids),
            )
        )
    ]
    for load in loads:
        load.start()
    greet_all()
    for load in loads:
        load.wait()

    order = (0, 1, 2, 3, 4, 5, 7, 8, 9)

    def own_block(b, carry):
        at = pl.ds(pl.multiple_of(b * BLK, BLK), BLK)
        for r, source in enumerate(order):
            own_cells[b * ROWS + r] = cells[source : source + 1, at]
        return carry

    lax.fori_loop(0, NCB, own_block, 0, unroll=8)

    def own_parts(b, carry):
        at = pl.ds(pl.multiple_of(b * BLK, BLK), BLK)
        for r in range(4):
            own_rows[b * 4 + r] = parts[r : r + 1, at]
        return carry

    lax.fori_loop(0, NBLK, own_parts, 0, unroll=8)

    for position, offset in enumerate(near_offsets):
        target = me + offset
        keep = jnp.where((target >= 0) & (target < DEV), 1.0, 0.0).astype(f32)
        for b in range(4):
            first = part_list[position, b] * 4
            for r in range(4):
                npick[position * 16 + b * 4 + r] = own_rows[first + r] * keep

    def choose0(d, carry):
        first = let_list[0, d] * ROWS
        for r in range(ROWS):
            chosen0[d * ROWS + r] = own_cells[first + r]
        return carry

    lax.fori_loop(0, DEV, choose0, 0, unroll=8)

    def choose_others(d, carry):
        count = let_count[0, d]
        for k, (chosen, base) in enumerate(
            ((chosen1, d * ONE), (chosen2, d * LATE), (chosen2, d * LATE + ROWS)), 1
        ):
            live = jnp.where(k < count, 1.0, 0.0).astype(f32)
            first = let_list[k, d] * ROWS
            for r in range(ROWS):
                chosen[base + r] = own_cells[first + r] * live
        chosen1[d * ONE + ROWS] = jnp.full((1, BLK), count.astype(f32))
        return carry

    lax.fori_loop(0, DEV, choose_others, 0, unroll=4)

    pl.semaphore_wait(barrier, DEV - 1)

    for position, offset in enumerate(near_offsets):
        d = lax.rem(me + offset + DEV, DEV)
        pltpu.make_async_remote_copy(
            npick.at[pl.ds(position * 16, 16)],
            npool.at[pl.ds(NBLK * 4 + position * 16, 16)],
            send_n.at[position],
            recv_n.at[position],
            device_id=(d // 8, lax.rem(d, 8)),
            device_id_type=MESH,
        ).start()

    phases = ((chosen0, pool0, OWN, ROWS), (chosen1, pool1, 0, ONE), (chosen2, pool2, 0, LATE))

    def send_all(phase):
        chosen, pool, base, rows = phases[phase]

        def send(ngx, ngy):
            pltpu.make_async_remote_copy(
                chosen.at[pl.ds((ngx * 8 + ngy) * rows, rows)],
                pool.at[pl.ds(base + me * rows, rows)],
                send_sem.at[phase],
                recv_sem.at[phase],
                device_id=(ngx, ngy),
                device_id_type=MESH,
            ).start()

        to_all(send)

    def wait_all(phase):
        chosen, pool, base, rows = phases[phase]
        pltpu.make_async_remote_copy(
            chosen.at[pl.ds(0, (DEV - 1) * rows)],
            pool.at[pl.ds(base, (DEV - 1) * rows)],
            send_sem.at[phase],
            recv_sem.at[phase],
            device_id=(gx, gy),
            device_id_type=MESH,
        ).wait()

    send_all(0)

    for r in range(ROWS):
        pool0[ZERO + r] = jnp.zeros((1, BLK), f32)

    lane = lax.broadcasted_iota(i32, (NBLK, BLK), 1)
    ids_v[...] = jnp.full((NBLK, BLK), -1, i32)
    ids_v[:, :LC] = cell_ids[...]
    ids = ids_v[...]
    remote = jnp.maximum(ids - NCB, 0)
    slot = remote & 3
    sender = remote >> 2
    listed = ids >= 0
    own = listed & (ids < NCB)
    far = ids >= NCB
    in0 = own | (far & (slot == 0))
    row0 = jnp.where(own, ids * ROWS, OWN + sender * ROWS)
    rank0 = ranks(in0, lane)
    packed = jnp.full((NBLK, BLK), ZERO, i32)
    for p in range(N0):
        packed = jnp.where(lane == p, ZERO - nth(in0, rank0, p + 1, ZERO - row0), packed)
    list_v[...] = packed
    to_list0 = pltpu.make_async_copy(list_v, list0, local_sem.at[7])
    to_list0.start()

    own_copies = [
        pltpu.make_async_copy(own_cells, pool0.at[pl.ds(0, OWN)], local_sem.at[0]),
        pltpu.make_async_copy(own_rows, npool.at[pl.ds(0, NBLK * 4)], local_sem.at[1]),
    ] + [
        pltpu.make_async_copy(
            chosen.at[pl.ds(me * rows, rows)],
            pool.at[pl.ds(base + me * rows, rows)],
            local_sem.at[2 + phase],
        )
        for phase, (chosen, pool, base, rows) in enumerate(phases)
    ]
    for copy in own_copies:
        copy.start()

    send_all(1)

    def spread(j, carry):
        at = pl.ds(pl.multiple_of(j * BLK, BLK), BLK)
        cols = jnp.transpose(parts[:, at])
        for c in range(3):
            t_ref[j * 3 + c] = jnp.broadcast_to(cols[:, c : c + 1], (BLK, BLK))
        return carry

    lax.fori_loop(0, NBLK, spread, 0, unroll=4)

    to_list0.wait()
    for copy in own_copies:
        copy.wait()
    for position in range(4):
        pltpu.make_async_remote_copy(
            npick.at[pl.ds(position * 16, 16)],
            npool.at[pl.ds(NBLK * 4 + position * 16, 16)],
            send_n.at[position],
            recv_n.at[position],
            device_id=(gx, gy),
            device_id_type=MESH,
        ).wait()

    def near_block(j, carry):
        acc[j] = jnp.zeros((4, BLK, BLK), f32)

        def item(i, inner):
            near_item(t_ref, j * 3, npool, [near_lists[i * 2 + k, j] for k in range(2)], acc.at[j])
            return inner

        lax.fori_loop(0, LP // 2, item, 0)
        return carry

    lax.fori_loop(0, NEAR_FIRST, near_block, 0)
    send_all(2)
    lax.fori_loop(NEAR_FIRST, NBLK, near_block, 0)

    wait_all(0)

    def block0(j, carry):
        cell_items(
            N0, lambda i: rows_of(pool0, list0[j, i], ROWS), t_ref, j * 3, acc.at[j]
        )
        return carry

    lax.fori_loop(0, NBLK, block0, 0)

    wait_all(1)

    row_lane = lax.broadcasted_iota(i32, (1, BLK), 1)

    def gather_counts(j, carry):
        counts = jnp.zeros((1, BLK), f32)
        for i in range(LC):
            sender_i = jnp.maximum(cell_lists[j, i] - NCB, 0) >> 2
            counts = jnp.where(row_lane == i, pool1[sender_i * ONE + ROWS], counts)
        count_v[j] = counts
        return carry

    lax.fori_loop(0, NBLK, gather_counts, 0, unroll=2)
    counts = count_v[...].reshape(NBLK, BLK)
    live = slot.astype(f32) < counts
    in1 = (in0 & (rank0 > N0)) | (far & (slot == 1) & live)
    in2 = far & (slot >= 2) & live
    row1 = jnp.where(in0, row0, ROWS0 + sender * ONE)
    row2 = sender * LATE + (slot - 2) * ROWS
    rank1 = ranks(in1, lane)
    rank2 = ranks(in2, lane)
    packed = jnp.full((NBLK, BLK), ZERO, i32)
    for p in range(N1):
        packed = jnp.where(lane == p, ZERO - nth(in1, rank1, p + 1, ZERO - row1), packed)
    list_v[...] = packed
    to_list1 = pltpu.make_async_copy(list_v, list1, local_sem.at[0])
    to_list1.start()
    n1 = jnp.sum(in1.astype(i32), axis=1, keepdims=True)
    n2 = jnp.sum(in2.astype(i32), axis=1, keepdims=True)
    packed = jnp.where(lane == 2 * LC, jnp.maximum(n1 - N1, 0), n2)
    for p in range(LC - N1):
        packed = jnp.where(lane == p, nth(in1, rank1, N1 + p + 1, row1), packed)
    for p in range(LC):
        packed = jnp.where(lane == LC + p, nth(in2, rank2, p + 1, row2), packed)
    left_lists[...] = packed
    to_list1.wait()

    def block1(j, carry):
        cell_items(
            N1, lambda i: rows_of_two(pool0, pool1, list1[j, i]), t_ref, j * 3, acc.at[j]
        )
        return carry

    lax.fori_loop(0, NBLK, block1, 0)

    wait_all(2)


def rest_kernel(lists, acc_in, t_ref, pool0, pool1, pool2, out, acc):
    def block(j, carry):
        cell_items(
            lists[j, 2 * LC],
            lambda i: rows_of_two(pool0, pool1, lists[j, i]),
            t_ref, j * 3, acc.at[j],
        )
        cell_items(
            lists[j, 2 * LC + 1],
            lambda i: rows_of(pool2, lists[j, LC + i], ROWS),
            t_ref, j * 3, acc.at[j],
        )
        return carry

    lax.fori_loop(0, NBLK, block, 0)

    def finish(j, carry):
        out[:, pl.ds(pl.multiple_of(j * BLK, BLK), BLK)] = lane_totals(acc.at[j])[:4]
        return carry

    lax.fori_loop(0, NBLK, finish, 0, unroll=8)


def body(particles, tree_cells, let_list, let_count, part_list, cell_lists, near_lists):
    smem = pl.BlockSpec(memory_space=pltpu.SMEM)
    vmem = pl.BlockSpec(memory_space=pltpu.VMEM)
    hbm = pl.BlockSpec(memory_space=pltpu.HBM)

    def rows(count):
        return pltpu.VMEM((count, 1, BLK), f32)

    acc_shape = (NBLK, 4, BLK, BLK)
    outs = pl.pallas_call(
        exchange_kernel,
        out_shape=(
            pltpu.VMEM(acc_shape, f32),
            pltpu.VMEM((3 * NBLK, BLK, BLK), f32),
            rows(ROWS0),
            rows(ROWS1),
            rows(ROWS2),
            pltpu.VMEM((NBLK, BLK), i32),
        ),
        in_specs=[hbm] * 7,
        out_specs=(vmem,) * 6,
        scratch_shapes=[
            pltpu.SMEM((4, DEV), i32),
            pltpu.SMEM((1, DEV), i32),
            pltpu.SMEM((4, 4), i32),
            pltpu.SMEM((LP, NBLK), i32),
            pltpu.SMEM((NBLK, LC), i32),
            pltpu.VMEM((NBLK, LC), i32),
            pltpu.VMEM(tree_cells.shape, f32),
            pltpu.VMEM(particles.shape, f32),
            rows(OWN),
            rows(NBLK * 4),
            rows(DEV * ROWS),
            rows(DEV * ONE),
            rows(DEV * LATE),
            rows(4 * 16),
            rows(2 * NBLK * 4),
            pltpu.VMEM((NBLK, BLK), i32),
            pltpu.VMEM((NBLK, 1, BLK), f32),
            pltpu.VMEM((NBLK, BLK), i32),
            pltpu.SMEM((NBLK, BLK), i32),
            pltpu.SMEM((NBLK, BLK), i32),
            pltpu.SemaphoreType.DMA((3,)),
            pltpu.SemaphoreType.DMA((3,)),
            pltpu.SemaphoreType.DMA((4,)),
            pltpu.SemaphoreType.DMA((4,)),
            pltpu.SemaphoreType.DMA((8,)),
        ],
        compiler_params=pltpu.CompilerParams(
            collective_id=0, has_side_effects=True, vmem_limit_bytes=24 << 20
        ),
        name="exchange",
    )(
        *[pltpu.with_memory_space_constraint(q, pltpu.HBM) for q in (jnp.transpose(let_list[0]), let_count, part_list[0],
        jnp.transpose(near_lists), cell_lists)], pltpu.with_memory_space_constraint(particles, pltpu.HBM), pltpu.with_memory_space_constraint(tree_cells, pltpu.HBM),
    )
    return pl.pallas_call(
        rest_kernel,
        out_shape=(jax.ShapeDtypeStruct(particles.shape, f32), pltpu.VMEM(acc_shape, f32)),
        in_specs=[smem] + [vmem] * 5,
        out_specs=(vmem, vmem),
        input_output_aliases={1: 1},
        compiler_params=pltpu.CompilerParams(vmem_limit_bytes=24 << 20),
        name="rest",
    )(outs[5], *outs[:5])[0]


def solution(mesh):
    return jax.shard_map(
        body,
        mesh=mesh,
        in_specs=(
            P(None, ("gx", "gy")),
            P(None, ("gx", "gy")),
            P(("gx", "gy"), None, None),
            P(("gx", "gy"), None),
            P(("gx", "gy"), None, None),
            P(("gx", "gy"), None),
            P(("gx", "gy"), None),
        ),
        out_specs=P(None, ("gx", "gy")),
        check_vma=False,
    )
```

profile of v0, /device:TPU:1, one launch (start us, length us, event | category | flops | bytes accessed | tf_op | source)
XLA Modules:
  0.0 50.8 jit_solution(10230651567223378155)
XLA Ops:
  0.0 40.2 %exchange.1 = (f32[16,4,128,128]{3,2,1,0:T(8,128)S(1)}, f32[48,128,128]{2,1,0:T(8,128)S(1)}, f32[1737,1,128]{2,1,0:T(1,128)S(1)}, f32[1280,1,128]{2,1,0:T(1,128)...) custom-call(s32[4,128]{1,0:T(4,128)} %bitcast.6, s32[1,128]{1,0:T(1,128)} %count_in.1, s32[4,4]{1,0:T(4,128)} %bitcast.7, ...), custom_call_target="tpu_custom_call" | custom-call | tf_op jit(solution)/shard_map/exchange/pallas_call | solution.py:466
  40.2 10.6 %rest.1 = (f32[4,2048]{1,0:T(4,128)}, f32[16,4,128,128]{3,2,1,0:T(8,128)S(1)}) custom-call(s32[16,128]{1,0:T(8,128)S(1)} %get-tuple-element.12.lists, f32[16,4,128,128]{3,2,1,0:T(8,128)S(1)} %get-tuple-element.13.acc_in, f32[48,128,128]{2,1,0:T(8,128)S(1)} %get-tuple-element.14.t_ref, ...), custom_call_target="tpu_custom_call", output_to_operand_aliasing={{1}: (1, {})} | custom-call | tf_op jit(solution)/shard_map/rest/pallas_call | solution.py:513
where the time goes:
time: 51.6 us; the launch traced here: 50.8 us
  Pallas kernels  50.8 us (98%)
    pallas_call x1, Pallas kernels, body(): pl.pallas_call(exchange_kernel, out_shape=(pltpu.VMEM(acc_shape, f32), pl...  40.2 us
    pallas_call x1, Pallas kernels, body(): pl.pallas_call(rest_kernel, out_shape=(jax.ShapeDtypeStruct(particles.sha...  10.6 us

commit v1 on v0

--- a/solution.py
+++ b/solution.py
@@ -162,7 +162,7 @@
             return carry
 
         batch(0, 0, True)
-        lax.fori_loop(1, 8, batch, 0)
+        lax.fori_loop(1, 8, batch, 0, unroll=7)
 
     barrier = pltpu.get_barrier_semaphore()
 

time: 51.6 us -> 50.7 us (0.983); the launches traced: 50.8 us -> 50.6 us
  no operation moved by 1% of the time
where the time goes in v1:
time: 50.7 us; the launch traced here: 50.6 us
  Pallas kernels  50.6 us (100%)
    pallas_call x1, Pallas kernels, body(): pl.pallas_call(exchange_kernel, out_shape=(pltpu.VMEM(acc_shape, f32), pl...  40 us
    pallas_call x1, Pallas kernels, body(): pl.pallas_call(rest_kernel, out_shape=(jax.ShapeDtypeStruct(particles.sha...  10.6 us

profile of v1, /device:TPU:1, one launch (start us, length us, event | category | flops | bytes accessed | tf_op | source)
XLA Modules:
  0.0 50.6 jit_solution(1194279210136126319)
XLA Ops:
  0.0 40.0 %exchange.1 = (f32[16,4,128,128]{3,2,1,0:T(8,128)S(1)}, f32[48,128,128]{2,1,0:T(8,128)S(1)}, f32[1737,1,128]{2,1,0:T(1,128)S(1)}, f32[1280,1,128]{2,1,0:T(1,128)...) custom-call(s32[4,128]{1,0:T(4,128)} %bitcast.6, s32[1,128]{1,0:T(1,128)} %count_in.1, s32[4,4]{1,0:T(4,128)} %bitcast.7, ...), custom_call_target="tpu_custom_call" | custom-call | tf_op jit(solution)/shard_map/exchange/pallas_call | solution.py:466
  40.0 10.6 %rest.1 = (f32[4,2048]{1,0:T(4,128)}, f32[16,4,128,128]{3,2,1,0:T(8,128)S(1)}) custom-call(s32[16,128]{1,0:T(8,128)S(1)} %get-tuple-element.12.lists, f32[16,4,128,128]{3,2,1,0:T(8,128)S(1)} %get-tuple-element.13.acc_in, f32[48,128,128]{2,1,0:T(8,128)S(1)} %get-tuple-element.14.t_ref, ...), custom_call_target="tpu_custom_call", output_to_operand_aliasing={{1}: (1, {})} | custom-call | tf_op jit(solution)/shard_map/rest/pallas_call | solution.py:513
